TPU v7x, 32 devices: a whole 2x2x4 slice. The times are simulated.
32 devices in a mesh: batch: 4 (over z), pb: 2 (over x), ka: 4 (over y, core).
Axes of the slice: x: 2, y: 2, z: 4, core: 2. Of those that a mesh axis runs over, the one named last changes fastest.
Arguments:
- inputs: bfloat16 [16, 1024, 768], P('batch', ('pb', 'ka')), may hold values from -6 to 6
- block_place: int32 [16, 8], P('batch'), may hold values from 0 to 7, each once within a row
- ln1_gain: float32 [768], replicated, may hold values from 0.1 to 1.9
- ln1_shift: float32 [768], replicated, may hold values from -3 to 3
- w_qkv: bfloat16 [768, 2304], replicated, may hold values from -0.21875 to 0.21875
- w_out: bfloat16 [768, 768], replicated, may hold values from -1.25 to 1.25
- ln2_gain: float32 [768], replicated, may hold values from 0.1 to 1.9
- ln2_shift: float32 [768], replicated, may hold values from -3 to 3
- w_up: bfloat16 [768, 3072], replicated, may hold values from -0.21875 to 0.21875
- w_down: bfloat16 [3072, 768], replicated, may hold values from -0.109375 to 0.109375
- cotangent: bfloat16 [16, 1024, 768], P('batch', ('pb', 'ka')), may hold values from -6 to 6
Outputs:
- outputs: bfloat16 [16, 1024, 768], P('batch', ('pb', 'ka'))
- grad_inputs: bfloat16 [16, 1024, 768], P('batch', ('pb', 'ka'))
- grad_qkv: float32 [768, 2304], P('batch', ('pb', 'ka'))
- grad_proj: float32 [768, 768], P('batch', ('pb', 'ka'))
- grad_up: float32 [768, 3072], P('batch', ('pb', 'ka'))
- grad_down: float32 [3072, 768], P('batch', ('pb', 'ka'))
- grad_norms: float32 [4, 768], P(None, ('pb', 'ka'))
Inputs may be any that keep to these rules, and one draw needn't show every extreme that they name: Each row of block_place lists every number 0 to 7 exactly once.
All inputs are finite; a program needn't handle non-finite values.
Results may differ from a plain program's by a relative error of at most 0.015.
The roundings to bfloat16 on the way count: a program that leaves them out, or rounds other values in their place, can miss the bound.
Values may be sent and summed in bfloat16 or wider, within the bound.
No kernel may reach another device: no remote copies, remote signals or barrier semaphores. Data moves between devices by JAX's collectives and lax.ppermute only.
A program may use at most 192 MiB of HBM per device.

v0:
```python
import jax
import jax.numpy as jnp
from jax import lax
from jax.sharding import PartitionSpec as P

HEADS = 12
HEAD = 64


norm_eps = 1e-05


def merged(part, axis, combine):
    gathered = jax.tree.map(lambda a: lax.all_gather(a, axis), part)

    def take(source):
        return jax.tree.map(lambda a: lax.dynamic_index_in_dim(a, source, 0, False), gathered)

    return lax.fori_loop(
        1, lax.axis_size(axis), lambda source, state: combine(state, take(source)), take(0)
    )


def norm_rows(values, gain_vec, shift_vec):
    average = jnp.mean(values, axis=-1, keepdims=True)
    centred = values - average
    spread = jnp.mean(centred * centred, axis=-1, keepdims=True)
    return centred * lax.rsqrt(spread + norm_eps) * gain_vec + shift_vec


def gelu_tanh(values):
    return jax.nn.gelu(values, approximate=True)


def split_heads(matrix):
    return matrix.reshape(matrix.shape[0], matrix.shape[1], HEADS, HEAD)


def combine_stats(former, latter):
    largest = jnp.maximum(former[0], latter[0])
    return (
        largest,
        former[1] * jnp.exp(former[0] - largest) + latter[1] * jnp.exp(latter[0] - largest),
    )


def tile_scores(query_heads, key_heads):
    return HEAD ** (-0.5) * jnp.einsum(
        "bqhe,bkhe->bhqk", query_heads, key_heads, preferred_element_type=jnp.float32
    )


def tile_weights(scores, visible, row_peak, row_total):
    sign_part = jnp.sign(scores)
    prob_part = (
        jnp.exp(jnp.where(visible, jnp.abs(scores) - row_peak[..., None], -1e30))
        / row_total[..., None]
    )
    return (sign_part, prob_part, sign_part * prob_part)


def shards(
    inputs,
    block_place,
    ln1_gain,
    ln1_shift,
    w_qkv,
    w_out,
    ln2_gain,
    ln2_shift,
    w_up,
    w_down,
    cotangent,
):
    seq_count, block_rows, model_width = inputs.shape
    key_devices = lax.axis_size("ka")
    query_devices = lax.axis_size("pb")
    query_index = lax.axis_index("pb")
    key_index = lax.axis_index("ka")
    offsets = jnp.arange(block_rows, dtype=jnp.int32)
    query_slots = query_index * key_devices + jnp.arange(key_devices, dtype=jnp.int32)
    key_slots = key_index + key_devices * jnp.arange(query_devices, dtype=jnp.int32)
    query_pos = (
        jnp.take(block_place, query_slots, axis=1)[:, :, None] * block_rows + offsets[None, None, :]
    ).reshape(seq_count, key_devices * block_rows)
    key_pos = (
        jnp.take(block_place, key_slots, axis=1)[:, :, None] * block_rows + offsets[None, None, :]
    ).reshape(seq_count, query_devices * block_rows)
    visible = key_pos[:, None, None, :] <= query_pos[:, None, :, None]
    source = inputs.astype(jnp.float32)
    normed1, first_back = jax.vjp(norm_rows, source, ln1_gain, ln1_shift)
    normed1 = normed1.astype(jnp.bfloat16)
    packed = jnp.einsum("btd,de->bte", normed1, w_qkv, preferred_element_type=jnp.float32).astype(
        jnp.bfloat16
    )
    query_half = lax.all_gather(packed[..., :model_width], "ka", axis=1, tiled=True)
    key_set, value_set = (
        lax.all_gather(packed[..., model_width : 2 * model_width], "pb", axis=1, tiled=True),
        lax.all_gather(packed[..., 2 * model_width :], "pb", axis=1, tiled=True),
    )
    query_heads = split_heads(query_half)
    key_heads = split_heads(key_set)
    value_heads = split_heads(value_set)
    scores = tile_scores(query_heads, key_heads)
    magnitude = jnp.abs(scores)
    local_peak = jnp.max(jnp.where(visible, magnitude, -1e30), axis=-1)
    local_sum = jnp.sum(
        jnp.exp(jnp.where(visible, magnitude - local_peak[..., None], -1e30)), axis=-1
    )
    row_peak, row_total = merged((local_peak, local_sum), "ka", combine_stats)
    sign_part, prob_part, signed = tile_weights(scores, visible, row_peak, row_total)
    weights_low = signed.astype(jnp.bfloat16)
    partial_value = jnp.einsum(
        "bhqk,bkhe->bqhe", weights_low, value_heads, preferred_element_type=jnp.float32
    )
    partial_value = partial_value.reshape(seq_count, key_devices * block_rows, model_width)
    attended = lax.psum_scatter(partial_value, "ka", scatter_dimension=1, tiled=True).astype(
        jnp.bfloat16
    )
    residual = source + jnp.einsum(
        "btd,de->bte", attended, w_out, preferred_element_type=jnp.float32
    )
    normed2, second_back = jax.vjp(norm_rows, residual, ln2_gain, ln2_shift)
    normed2 = normed2.astype(jnp.bfloat16)
    pre_act = jnp.einsum("btd,df->btf", normed2, w_up, preferred_element_type=jnp.float32)
    active, gelu_back = jax.vjp(gelu_tanh, pre_act)
    active = active.astype(jnp.bfloat16)
    outputs = (
        residual + jnp.einsum("btf,fd->btd", active, w_down, preferred_element_type=jnp.float32)
    ).astype(jnp.bfloat16)
    grad_down = jnp.einsum("btf,btd->fd", active, cotangent, preferred_element_type=jnp.float32)
    grad_act = jnp.einsum("btd,fd->btf", cotangent, w_down, preferred_element_type=jnp.float32)
    grad_pre = gelu_back(grad_act)[0].astype(jnp.bfloat16)
    grad_up = jnp.einsum("btd,btf->df", normed2, grad_pre, preferred_element_type=jnp.float32)
    grad_normed2 = jnp.einsum("btf,df->btd", grad_pre, w_up, preferred_element_type=jnp.float32)
    grad_res, grad_gain2, grad_shift2 = second_back(grad_normed2)
    grad_res = grad_res + cotangent.astype(jnp.float32)
    grad_z = grad_res.astype(jnp.bfloat16)
    grad_proj = jnp.einsum("btd,bte->de", attended, grad_z, preferred_element_type=jnp.float32)
    grad_att = jnp.einsum("bte,de->btd", grad_z, w_out, preferred_element_type=jnp.float32).astype(
        jnp.bfloat16
    )
    grad_half = lax.all_gather(grad_att, "ka", axis=1, tiled=True)
    grad_heads = split_heads(grad_half)
    scores = tile_scores(query_heads, key_heads)
    sign_part, prob_part, signed = tile_weights(scores, visible, row_peak, row_total)
    weights_low = signed.astype(jnp.bfloat16)
    grad_weights = jnp.einsum(
        "bqhe,bkhe->bhqk", grad_heads, value_heads, preferred_element_type=jnp.float32
    )
    delta_rows = lax.psum(jnp.sum(signed * grad_weights, axis=-1), "ka")
    grad_scores = (
        sign_part * prob_part * (sign_part * grad_weights - delta_rows[..., None])
    ).astype(jnp.bfloat16)
    factor = HEAD ** (-0.5)
    grad_q = factor * jnp.einsum(
        "bhqk,bkhe->bqhe", grad_scores, key_heads, preferred_element_type=jnp.float32
    )
    grad_k = factor * jnp.einsum(
        "bhqk,bqhe->bkhe", grad_scores, query_heads, preferred_element_type=jnp.float32
    )
    grad_v = jnp.einsum(
        "bhqk,bqhe->bkhe", weights_low, grad_heads, preferred_element_type=jnp.float32
    )
    query_grad = lax.psum_scatter(
        grad_q.reshape(seq_count, key_devices * block_rows, model_width).astype(jnp.bfloat16),
        "ka",
        scatter_dimension=1,
        tiled=True,
    ).astype(jnp.float32)
    key_grad, value_grad = (
        lax.psum_scatter(
            grad_k.reshape(seq_count, query_devices * block_rows, model_width).astype(jnp.bfloat16),
            "pb",
            scatter_dimension=1,
            tiled=True,
        ).astype(jnp.float32),
        lax.psum_scatter(
            grad_v.reshape(seq_count, query_devices * block_rows, model_width).astype(jnp.bfloat16),
            "pb",
            scatter_dimension=1,
            tiled=True,
        ).astype(jnp.float32),
    )
    grad_packed = jnp.concatenate([query_grad, key_grad, value_grad], axis=-1).astype(jnp.bfloat16)
    grad_qkv = jnp.einsum("btd,bte->de", normed1, grad_packed, preferred_element_type=jnp.float32)
    grad_normed1 = jnp.einsum("bte,de->btd", grad_packed, w_qkv, preferred_element_type=jnp.float32)
    grad_source, grad_gain1, grad_shift1 = first_back(grad_normed1)
    grad_inputs = (grad_res + grad_source).astype(jnp.bfloat16)
    norm_local = jnp.stack([grad_gain1, grad_shift1, grad_gain2, grad_shift2])
    widened = (
        lax.psum_scatter(
            grad_qkv.astype(jnp.bfloat16), "batch", scatter_dimension=0, tiled=True
        ).astype(jnp.float32),
        lax.psum_scatter(
            grad_proj.astype(jnp.bfloat16), "batch", scatter_dimension=0, tiled=True
        ).astype(jnp.float32),
        lax.psum_scatter(
            grad_up.astype(jnp.bfloat16), "batch", scatter_dimension=0, tiled=True
        ).astype(jnp.float32),
        lax.psum_scatter(
            grad_down.astype(jnp.bfloat16), "batch", scatter_dimension=0, tiled=True
        ).astype(jnp.float32),
    )
    summed = (
        lax.psum_scatter(
            widened[0].astype(jnp.bfloat16), ("pb", "ka"), scatter_dimension=1, tiled=True
        ).astype(jnp.float32),
        lax.psum_scatter(
            widened[1].astype(jnp.bfloat16), ("pb", "ka"), scatter_dimension=1, tiled=True
        ).astype(jnp.float32),
        lax.psum_scatter(
            widened[2].astype(jnp.bfloat16), ("pb", "ka"), scatter_dimension=1, tiled=True
        ).astype(jnp.float32),
        lax.psum_scatter(
            widened[3].astype(jnp.bfloat16), ("pb", "ka"), scatter_dimension=1, tiled=True
        ).astype(jnp.float32),
        lax.psum_scatter(
            norm_local.astype(jnp.bfloat16), ("pb", "ka"), scatter_dimension=1, tiled=True
        ).astype(jnp.float32),
    )
    norm_sum = lax.psum(summed[4], "batch")
    return (outputs, grad_inputs, summed[0], summed[1], summed[2], summed[3], norm_sum)


def solution(mesh):
    placed = (
        P("batch", ("pb", "ka"), None),
        P("batch", None),
        P(),
        P(),
        P(),
        P(),
        P(),
        P(),
        P(),
        P(),
        P("batch", ("pb", "ka"), None),
    )
    return jax.shard_map(
        shards,
        mesh=mesh,
        in_specs=placed,
        out_specs=(
            P("batch", ("pb", "ka"), None),
            P("batch", ("pb", "ka"), None),
            P("batch", ("pb", "ka")),
            P("batch", ("pb", "ka")),
            P("batch", ("pb", "ka")),
            P("batch", ("pb", "ka")),
            P(None, ("pb", "ka")),
        ),
        check_vma=False,
    )
```

profile of v0, /device:TPU:0, one launch (start us, length us, event | category | flops | bytes accessed | tf_op | source)
XLA Modules:
  0.0 959.3 jit_solution(2006295980375979858)
XLA Ops:
  10.8 3.3 convolution_convert_fusion
  20.1 25.6 %all-gather.11.cloned.1.call-done = bf16[4,256,768]{2,1,0:T(8,128)(2,1)} async-done(((bf16[4,128,768]{2,1,0:T(8,128)(2,1)}), bf16[4,256,768]{2,1,0:T(8,128)(2,1)}) %all-gather.11.cloned.1.call-update) | async-done | bytes 1572880 | tf_op jit(solution)/shard_map/all_gather | solution.py:98
  45.7 2.6 copy.64
  48.3 26.2 %all-gather.7.cloned.1.call-done = bf16[4,256,768]{2,1,0:T(8,128)(2,1)} async-done(((bf16[4,128,768]{2,1,0:T(8,128)(2,1)}), bf16[4,256,768]{2,1,0:T(8,128)(2,1)}) %all-gather.7.cloned.1.call-update) | async-done | bytes 1572880 | tf_op jit(solution)/shard_map/all_gather | solution.py:99
  74.5 2.6 copy.62
  77.0 28.1 %all-gather.9.cloned.1.call-done = bf16[4,512,768]{2,1,0:T(8,128)(2,1)} async-done(((bf16[4,128,768]{2,1,0:T(8,128)(2,1)}), bf16[4,512,768]{2,1,0:T(8,128)(2,1)}) %all-gather.9.cloned.1.call-update) | async-done | bytes 3145744 | tf_op jit(solution)/shard_map/all_gather | solution.py:96
  105.2 4.7 copy.63
  109.9 13.1 %select_reduce_fusion = (f32[4,12,512]{2,1,0:T(8,128)S(1)}, f32[4,12,512,256]{2,3,1,0:T(8,128)}) fusion(pred[4,512,256]{1,2,0:T(8,128)(4,1)} %broadcast_compare_fusion, bf16[4,512,12,64]{1,3,2,0:T(8,128)(2,1)} %bitcast.118, bf16[4,256,12,64]{1,3,2,0:T(8,128)(2,1)} %bitcast.123), kind=kOutput, calls=%fused_computation.11 | convolution fusion | flops 830447616 | bytes 30507008 | tf_op jit(solution)/shard_map/bqhe,bkhe->bhqk/dot_general | solution.py:48
  123.0 7.2 all-gather
  130.1 11.7 %exponential_reduce_fusion = f32[4,12,512]{2,1,0:T(8,128)S(1)} fusion(f32[4,12,512,256]{2,3,1,0:T(8,128)} %get-tuple-element.187, f32[4,12,512]{2,1,0:T(8,128)S(1)} %get-tuple-element.186, pred[4,512,256]{1,2,0:T(8,128)(4,1)S(1)} %copy-done.7), kind=kLoop, calls=%fused_computation.10 | loop fusion | flops 31432704 | bytes 25886720 | tf_op jit(solution)/shard_map/reduce_sum | solution.py:107
  142.5 7.5 all-gather.1
  150.8 5.5 while.17
  150.8 1.8 fusion.76
  152.6 1.8 fusion.76
  154.4 1.8 fusion.76
  156.3 21.3 %fusion.11 = f32[4,12,64,512]{3,2,1,0:T(8,128)} fusion(bf16[4,256,12,64]{1,3,2,0:T(8,128)(2,1)} %bitcast.132, f32[4,12,512,256]{2,3,1,0:T(8,128)} %get-tuple-element.187, f32[4,12,512]{2,1,0:T(8,128)} %get-tuple-element.141, f32[4,12,512]{2,1,0:T(8,128)} %get-tuple-element.140, pred[4,512,256]{1,2,0:T(8,128)(4,1)} %broadcast_compare_fusion), kind=kOutput, calls=%fused_computation.28 | convolution fusion | flops 855638016 | bytes 33751040 | tf_op jit(solution)/shard_map/bhqk,bkhe->bqhe/dot_general | solution.py:113
  178.0 57.7 %reduce-scatter.24.cloned.1.call-done = f32[4,128,768]{1,2,0:T(8,128)} async-done(((f32[4,512,768]{1,2,0:T(8,128)}), f32[4,128,768]{1,2,0:T(8,128)}) %reduce-scatter.24.cloned.1.call-update) | async-done | bytes 1572880 | tf_op jit(solution)/shard_map/reduce_scatter | solution.py:117
  235.7 3.0 fusion.56
  239.1 4.9 fusion.19
  244.1 6.2 fusion.8
  250.3 3.5 multiply_reduce_fusion.1
  256.9 1.7 convolution_convert_fusion.1
  259.1 28.1 %all-gather.13.cloned.1.call-done = bf16[4,512,768]{2,1,0:T(8,128)(2,1)} async-done(((bf16[4,128,768]{2,1,0:T(8,128)(2,1)}), bf16[4,512,768]{2,1,0:T(8,128)(2,1)}) %all-gather.13.cloned.1.call-update) | async-done | bytes 3145744 | tf_op jit(solution)/shard_map/all_gather | solution.py:143
  287.3 4.7 copy.71
  291.9 27.0 %multiply_reduce_fusion = (f32[4,12,512]{2,1,0:T(8,128)}, f32[4,12,512,256]{2,3,1,0:T(8,128)}) fusion(f32[4,12,512]{2,1,0:T(8,128)} %get-tuple-element.141, f32[4,12,512]{2,1,0:T(8,128)} %get-tuple-element.140, pred[4,512,256]{1,2,0:T(8,128)(4,1)} %broadcast_compare_fusion, f32[4,12,512,256]{2,3,1,0:T(8,128)} %get-tuple-element.187, ...), kind=kOutput, calls=%fused_computation.8 | convolution fusion | flops 861904896 | bytes 55869440 | tf_op jit(solution)/shard_map/bqhe,bkhe->bhqk/dot_general | solution.py:148
  319.2 31.7 %all-reduce.2.cloned.1.call-done = f32[4,12,512]{2,1,0:T(8,128)} async-done(((f32[4,12,512]{2,1,0:T(8,128)}), f32[4,12,512]{2,1,0:T(8,128)}) %all-reduce.2.cloned.1.call-update) | async-done | bytes 98320 | tf_op jit(solution)/shard_map/psum | solution.py:151
  350.9 21.8 %multiply_convert_fusion = bf16[4,12,512,256]{2,3,1,0:T(8,128)(2,1)S(1)} fusion(f32[4,12,512,256]{2,3,1,0:T(8,128)} %get-tuple-element.192, f32[4,12,512,256]{2,3,1,0:T(8,128)} %get-tuple-element.187, f32[4,12,512]{2,1,0:T(8,128)} %all-reduce.2.cloned.1.call-done, f32[4,12,512]{2,1,0:T(8,128)} %get-tuple-element.141, f32[4,12,512]{2,1,0:T(8,128)} %get-tuple-element.140, ...), kind=kLoop, calls=%fused_computation.7 | loop fusion | flops 69206016 | bytes 63733760 | tf_op jit(solution)/shard_map/convert_element_type | solution.py:154
  372.7 4.5 multiply_convert_fusion.1
  378.3 4.7 copy.73
  383.0 10.7 %multiply_convert_fusion.3 = bf16[4,12,64,256]{3,2,1,0:T(8,128)(2,1)} fusion(bf16[4,512,12,64]{1,3,2,0:T(8,128)(2,1)} %bitcast.119, bf16[4,12,512,256]{2,3,1,0:T(8,128)(2,1)} %copy-done.1), kind=kOutput, calls=%fused_computation.42 | convolution fusion | flops 806879232 | bytes 17301504 | tf_op jit(solution)/shard_map/bhqk,bqhe->bkhe/dot_general | solution.py:159
  393.7 2.6 copy.75
  396.5 22.1 %fusion.32 = bf16[4,12,64,256]{3,2,1,0:T(8,128)(2,1)} fusion(bf16[4,512,12,64]{1,3,2,0:T(8,128)(2,1)} %bitcast.131, f32[4,12,512,256]{2,3,1,0:T(8,128)} %get-tuple-element.187, f32[4,12,512]{2,1,0:T(8,128)} %get-tuple-element.141, f32[4,12,512]{2,1,0:T(8,128)} %get-tuple-element.140, pred[4,512,256]{1,2,0:T(8,128)(4,1)} %broadcast_compare_fusion), kind=kOutput, calls=%fused_computation.55 | convolution fusion | flops 856424448 | bytes 30605312 | tf_op jit(solution)/shard_map/bhqk,bqhe->bkhe/dot_general | solution.py:162
  418.7 2.6 copy.77
  421.3 3.4 bitcast_convert_fusion.3
  424.8 8.4 bitcast_convert_fusion
  434.0 7.4 bitcast_convert_fusion.1
  441.5 2.2 constant_dynamic-update-slice_fusion.2
  443.7 5.6 reduce-scatter.28.cloned.1.call-done
  449.3 2.1 constant_dynamic-update-slice_fusion.1
  451.4 26.3 %reduce-scatter.30.cloned.1.call-done = bf16[4,128,768]{2,1,0:T(8,128)(2,1)} async-done(((bf16[4,256,768]{2,1,0:T(8,128)(2,1)}), bf16[4,128,768]{2,1,0:T(8,128)(2,1)}) %reduce-scatter.30.cloned.1.call-update) | async-done | bytes 786448 | tf_op jit(solution)/shard_map/reduce_scatter | solution.py:178
  477.7 2.1 constant_dynamic-update-slice_fusion
  479.8 6.0 bitcast_convert_fusion.2
  487.8 21.5 %reduce-scatter.34.cloned.1.call-done = bf16[192,768]{1,0:T(8,128)(2,1)} async-done(((bf16[768,768]{1,0:T(8,128)(2,1)}), bf16[192,768]{1,0:T(8,128)(2,1)}) %reduce-scatter.34.cloned.1.call-update) | async-done | bytes 294928 | tf_op jit(solution)/shard_map/reduce_scatter | solution.py:195
  509.3 1.9 copy.92
  511.3 4.0 fusion.39
  517.7 77.7 %reduce-scatter.38.cloned.1.call-done = bf16[768,768]{1,0:T(8,128)(2,1)} async-done(((bf16[3072,768]{1,0:T(8,128)(2,1)}), bf16[768,768]{1,0:T(8,128)(2,1)}) %reduce-scatter.38.cloned.1.call-update) | async-done | bytes 1179664 | tf_op jit(solution)/shard_map/reduce_scatter | solution.py:201
  595.5 2.4 copy.96
  597.9 85.5 %reduce-scatter.36.cloned.1.call-done = bf16[192,3072]{1,0:T(8,128)(2,1)} async-done(((bf16[768,3072]{1,0:T(8,128)(2,1)}), bf16[192,3072]{1,0:T(8,128)(2,1)}) %reduce-scatter.36.cloned.1.call-update) | async-done | bytes 1179664 | tf_op jit(solution)/shard_map/reduce_scatter | solution.py:198
  683.5 2.5 copy.94
  686.4 66.5 %reduce-scatter.32.cloned.1.call-done = bf16[192,2304]{1,0:T(8,128)(2,1)} async-done(((bf16[768,2304]{1,0:T(8,128)(2,1)}), bf16[192,2304]{1,0:T(8,128)(2,1)}) %reduce-scatter.32.cloned.1.call-update) | async-done | bytes 884752 | tf_op jit(solution)/shard_map/reduce_scatter | solution.py:192
  752.9 2.3 copy.90
  755.2 9.3 add_convert_fusion.1
  764.5 25.9 %reduce-scatter.42.cloned.1.call-done = bf16[96,192]{1,0:T(8,128)(2,1)} async-done(((bf16[768,192]{1,0:T(8,128)(2,1)}), bf16[96,192]{1,0:T(8,128)(2,1)}) %reduce-scatter.42.cloned.1.call-update) | async-done | bytes 36880
  794.1 3.9 add_convert_fusion
  798.0 29.6 %reduce-scatter.48.cloned.1.call-done = bf16[96,4]{1,0:T(8,128)(2,1)} async-done(((bf16[768,4]{1,0:T(8,128)(2,1)}), bf16[96,4]{1,0:T(8,128)(2,1)}) %reduce-scatter.48.cloned.1.call-update) | async-done | bytes 784
  828.4 12.2 %psum.15 = f32[4,96]{1,0:T(4,128)} all-reduce(bf16[4,96]{1,0:T(4,128)(2,1)S(1)} %copy.99), channel_id=1, replica_groups=mesh['batch'=4,'pb'=2,'ka'=4] {'batch'}, use_global_device_ids=true, to_apply=%region_31.32 | all-reduce | flops 384 | bytes 2304 | tf_op jit(solution)/shard_map/psum | solution.py:222
  840.6 26.7 %reduce-scatter.46.cloned.1.call-done = bf16[96,768]{1,0:T(8,128)(2,1)} async-done(((bf16[768,768]{1,0:T(8,128)(2,1)}), bf16[96,768]{1,0:T(8,128)(2,1)}) %reduce-scatter.46.cloned.1.call-update) | async-done | bytes 147472
  867.4 1.7 copy.97
  869.1 1.8 copy.81
  870.9 38.0 %reduce-scatter.44.cloned.1.call-done = bf16[384,192]{1,0:T(8,128)(2,1)} async-done(((bf16[3072,192]{1,0:T(8,128)(2,1)}), bf16[384,192]{1,0:T(8,128)(2,1)}) %reduce-scatter.44.cloned.1.call-update) | async-done | bytes 147472
  908.8 1.7 copy.95
  910.6 1.6 convert_element_type.138
  912.2 36.4 %reduce-scatter.40.cloned.1.call-done = bf16[288,192]{1,0:T(8,128)(2,1)} async-done(((bf16[2304,192]{1,0:T(8,128)(2,1)}), bf16[288,192]{1,0:T(8,128)(2,1)}) %reduce-scatter.40.cloned.1.call-update) | async-done | bytes 110608
  948.6 1.7 copy.91
  (171 shorter events, 28.5 us)
Async XLA Ops:
  7.2 3.6 copy-start
  7.2 38.5 %all-gather.11.cloned.1.call-start = ((), (), s32[]{:S(2)}) async-start(), calls=%async_computation.15 | async-start | bytes 2359296 | tf_op jit(solution)/shard_map/all_gather | solution.py:98
  8.7 5.4 copy-start.13
  10.2 0.6 copy-start.20
  10.8 3.3 copy-start.15
  14.1 3.1 copy-start.32
  15.6 58.8 %all-gather.7.cloned.1.call-start = ((), (), s32[]{:S(2)}) async-start(), calls=%async_computation.13 | async-start | bytes 2359296 | tf_op jit(solution)/shard_map/all_gather | solution.py:99
  16.4 88.8 %all-gather.9.cloned.1.call-start = ((), (), s32[]{:S(2)}) async-start(), calls=%async_computation.14 | async-start | bytes 3932160 | tf_op jit(solution)/shard_map/all_gather | solution.py:96
  17.1 218.6 %reduce-scatter.24.cloned.1.call-start = ((), (), s32[]{:S(2)}) async-start(), calls=%async_computation.16 | async-start | bytes 7864320 | tf_op jit(solution)/shard_map/reduce_scatter | solution.py:117
  109.9 20.3 %copy-start.7 = (pred[4,512,256]{1,2,0:T(8,128)(4,1)S(1)}, pred[4,512,256]{1,2,0:T(8,128)(4,1)}, u32[]{:S(2)}) copy-start(pred[4,512,256]{1,2,0:T(8,128)(4,1)} %broadcast_compare_fusion) | copy-start | bytes 1572868
  130.1 11.7 %copy-start.8 = (f32[16,12,512]{2,1,0:T(8,128)}, f32[16,12,512]{2,1,0:T(8,128)S(1)}, u32[]{:S(2)}) copy-start(f32[16,12,512]{2,1,0:T(8,128)S(1)} %all-gather) | copy-start | bytes 1179652
  149.9 0.8 copy-start.9
  177.6 61.4 %copy-start.30 = (f32[768]{0:T(1024)S(1)}, f32[768]{0:T(1024)}, u32[]{:S(2)}) copy-start(f32[768]{0:T(1024)} %param.19) | copy-start | bytes 9220
  177.7 61.4 %copy-start.34 = (f32[768]{0:T(1024)S(1)}, f32[768]{0:T(1024)}, u32[]{:S(2)}) copy-start(f32[768]{0:T(1024)} %param.20) | copy-start | bytes 9220
  177.7 109.6 %all-gather.13.cloned.1.call-start = ((), (), s32[]{:S(2)}) async-start(), calls=%async_computation.17 | async-start | bytes 3932160 | tf_op jit(solution)/shard_map/all_gather | solution.py:143
  235.7 8.4 slice-start.2
  238.7 15.2 %copy-start.3 = (f32[4,128,768]{2,1,0:T(8,128)}, f32[4,128,768]{2,1,0:T(8,128)S(1)}, u32[]{:S(2)}) copy-start(f32[4,128,768]{2,1,0:T(8,128)S(1)} %get-tuple-element.189) | copy-start | bytes 4718596
  238.7 15.2 %copy-start.18 = (f32[4,128]{1,0:T(4,128)}, f32[4,128]{1,0:T(4,128)S(1)}, u32[]{:S(2)}) copy-start(f32[4,128]{1,0:T(4,128)S(1)} %broadcast_multiply_fusion) | copy-start | bytes 6148
  239.1 14.8 %copy-start.28 = (f32[4,128]{1,0:T(4,128)}, f32[4,128]{1,0:T(4,128)S(1)}, u32[]{:S(2)}) copy-start(f32[4,128]{1,0:T(4,128)S(1)} %fusion.51) | copy-start | bytes 6148
  239.1 5.0 copy-start.11
  239.1 5.0 slice-start.3
  239.1 11.2 %slice-start = ((s8[4718592]{0:T(1024)(128)(4,1)}), s8[4194304]{0:T(1024)(128)(4,1)S(1)}, s32[]{:S(2)}) async-start(s8[4718592]{0:T(1024)(128)(4,1)} %bitcast.142), calls=%async_computation.31 | async-start | bytes 8388608
  244.1 6.2 copy-start.37
  244.1 6.2 slice-start.1
  250.3 3.5 copy-start.38
  253.9 3.0 copy-start.12
  254.5 1.2 copy-start.4
  254.6 1.4 copy-start.22
  256.0 0.9 copy-start.10
  258.6 92.3 %all-reduce.2.cloned.1.call-start = ((), (), s32[]{:S(2)}) async-start(), calls=%async_computation.18 | async-start | bytes 262144 | tf_op jit(solution)/shard_map/psum | solution.py:151
  319.0 122.5 %reduce-scatter.26.cloned.1.call-start = ((), (), s32[]{:S(2)}) async-start(), calls=%async_computation.19 | async-start | bytes 3932160 | tf_op jit(solution)/shard_map/reduce_scatter | solution.py:165
  350.9 21.8 %copy-start.5 = (bf16[4,256,768]{1,2,0:T(8,128)(2,1)S(1)}, bf16[4,256,768]{1,2,0:T(8,128)(2,1)}, u32[]{:S(2)}) copy-start(bf16[4,256,768]{1,2,0:T(8,128)(2,1)} %copy.64) | copy-start | bytes 4718596
  372.7 5.5 copy-start.1
  382.9 66.3 %reduce-scatter.28.cloned.1.call-start = ((), (), s32[]{:S(2)}) async-start(), calls=%async_computation.20 | async-start | bytes 2359296 | tf_op jit(solution)/shard_map/reduce_scatter | solution.py:172
  396.3 81.4 %reduce-scatter.30.cloned.1.call-start = ((), (), s32[]{:S(2)}) async-start(), calls=%async_computation.21 | async-start | bytes 2359296 | tf_op jit(solution)/shard_map/reduce_scatter | solution.py:178
  421.3 88.0 %reduce-scatter.34.cloned.1.call-start = ((), (), s32[]{:S(2)}) async-start(), calls=%async_computation.23 | async-start | bytes 1474560 | tf_op jit(solution)/shard_map/reduce_scatter | solution.py:195
  424.8 170.7 %reduce-scatter.38.cloned.1.call-start = ((), (), s32[]{:S(2)}) async-start(), calls=%async_computation.25 | async-start | bytes 5898240 | tf_op jit(solution)/shard_map/reduce_scatter | solution.py:201
  433.3 0.7 copy-start.19
  433.3 0.7 copy-start.29
  433.3 0.7 copy-start.31
  433.3 0.7 copy-start.35
  433.3 250.2 %reduce-scatter.36.cloned.1.call-start = ((), (), s32[]{:S(2)}) async-start(), calls=%async_computation.24 | async-start | bytes 5898240 | tf_op jit(solution)/shard_map/reduce_scatter | solution.py:198
  441.4 38.4 %copy-start.14 = (f32[4,128]{1,0:T(4,128)S(1)}, f32[4,128]{1,0:T(4,128)}, u32[]{:S(2)}) copy-start(f32[4,128]{1,0:T(4,128)} %copy-done.13) | copy-start | bytes 6148
  441.4 38.4 %copy-start.16 = (f32[4,128]{1,0:T(4,128)S(1)}, f32[4,128]{1,0:T(4,128)}, u32[]{:S(2)}) copy-start(f32[4,128]{1,0:T(4,128)} %copy-done.15) | copy-start | bytes 6148
  441.4 38.4 %copy-start.24 = (f32[768]{0:T(1024)S(1)}, f32[768]{0:T(1024)}, u32[]{:S(2)}) copy-start(f32[768]{0:T(1024)} %param.15) | copy-start | bytes 9220
  441.4 38.4 %copy-start.36 = (f32[768]{0:T(1024)S(1)}, f32[768]{0:T(1024)}, u32[]{:S(2)}) copy-start(f32[768]{0:T(1024)} %param.16) | copy-start | bytes 9220
  441.4 311.5 %reduce-scatter.32.cloned.1.call-start = ((), (), s32[]{:S(2)}) async-start(), calls=%async_computation.22 | async-start | bytes 4423680 | tf_op jit(solution)/shard_map/reduce_scatter | solution.py:192
  485.8 1.3 copy-start.33
  485.9 304.6 %reduce-scatter.42.cloned.1.call-start = ((), (), s32[]{:S(2)}) async-start(), calls=%async_computation.27 | async-start | bytes 442368
  511.2 4.1 copy-start.21
  511.2 316.4 %reduce-scatter.48.cloned.1.call-start = ((), (), s32[]{:S(2)}) async-start(), calls=%async_computation.30 | async-start | bytes 221184
  511.2 4.1 copy-start.2
  511.2 4.1 copy-start.25
  511.3 5.5 copy-start.26
  511.3 5.5 copy-start.27
  515.3 1.5 copy-start.6
  517.7 349.7 %reduce-scatter.46.cloned.1.call-start = ((), (), s32[]{:S(2)}) async-start(), calls=%async_computation.29 | async-start | bytes 1327104
  597.9 310.9 %reduce-scatter.44.cloned.1.call-start = ((), (), s32[]{:S(2)}) async-start(), calls=%async_computation.28 | async-start | bytes 1769472
  686.0 262.6 %reduce-scatter.40.cloned.1.call-start = ((), (), s32[]{:S(2)}) async-start(), calls=%async_computation.26 | async-start | bytes 1327104
  755.2 38.9 %copy-start.17 = (f32[4,128]{1,0:T(4,128)S(1)}, f32[4,128]{1,0:T(4,128)}, u32[]{:S(2)}) copy-start(f32[4,128]{1,0:T(4,128)} %copy-done.15) | copy-start | bytes 6148
  755.2 38.9 %copy-start.23 = (f32[4,128]{1,0:T(4,128)S(1)}, f32[4,128]{1,0:T(4,128)}, u32[]{:S(2)}) copy-start(f32[4,128]{1,0:T(4,128)} %copy-done.22) | copy-start | bytes 6148
Sparse Core Ops, SparseCore 0:
  15.8 29.8 all-gather.10
  47.2 27.1 all-gather.6
  76.6 28.5 all-gather.8
  177.8 57.8 reduce-scatter.23
  258.7 28.4 all-gather.12
  319.1 31.7 all-reduce.1
  383.1 37.7 reduce-scatter.25
  423.1 26.1 reduce-scatter.27
  451.5 26.1 reduce-scatter.29
  479.9 29.3 reduce-scatter.33
  511.6 83.8 reduce-scatter.37
  597.6 85.7 reduce-scatter.35
  685.8 67.0 reduce-scatter.31
  756.4 34.0 reduce-scatter.41
  793.9 33.6 reduce-scatter.47
  830.6 36.6 reduce-scatter.45
  870.5 38.2 reduce-scatter.43
  911.9 36.6 reduce-scatter.39
where the time goes:
time: 967 us; the launch traced here: 959 us
  waiting for transfers between devices  639 us (66%)
  matrix products  160 us (17%)
  local copies, waits for them, and re-layouts  60.4 us (6%)
  other arithmetic  55.3 us (6%)
  blocking collectives  26.9 us (3%)
  between operations  15.4 us (2%)
    unnamed x23, waiting for transfers between devices  158 us
    reduce_scatter x1, waiting for transfers between devices, shards(): lax.psum_scatter(grad_up.astype(jnp.bfloat16), 'batch', scatter_dimension...  85.5 us
    reduce_scatter x1, waiting for transfers between devices, shards(): lax.psum_scatter(grad_down.astype(jnp.bfloat16), 'batch', scatter_dimensi...  77.7 us
    reduce_scatter x1, waiting for transfers between devices, shards(): lax.psum_scatter(grad_qkv.astype(jnp.bfloat16), 'batch', scatter_dimensio...  66.5 us
    reduce_scatter x1, waiting for transfers between devices, shards(): lax.psum_scatter(partial_value, 'ka', scatter_dimension=1, tiled=True)  57.7 us
    psum x1, waiting for transfers between devices, shards(): delta_rows = lax.psum(jnp.sum(signed * grad_weights, axis=-1), 'ka')  31.7 us
    all_gather x1, waiting for transfers between devices, shards(): grad_half = lax.all_gather(grad_att, 'ka', axis=1, tiled=True)  28.1 us
    all_gather x1, waiting for transfers between devices, shards(): lax.all_gather(packed[..., :model_width], 'ka', axis=1, tiled=True)  28.1 us
  transfers between devices with their start and end apart: 18, of which 17 were waited for; matrix products, arithmetic and copies ran while one was open for 12% of the time, Pallas kernels for 0%

commit v1 on v0

v1 whole, which is shorter than its diff:
```python
import functools

import jax
import jax.numpy as jnp
from jax import lax
from jax.experimental import pallas as pl
from jax.experimental.pallas import tpu as pltpu
from jax.sharding import PartitionSpec as P

HEADS = 12
HEAD = 64
PAIR = 2 * HEAD
QTILE = 256
SCALE = HEAD ** (-0.5)
HUGE = 3e38
HIDDEN = -1e30

norm_eps = 1e-05
BF16 = jnp.bfloat16
F32 = jnp.float32


def norm_rows(values, gain_vec, shift_vec):
    average = jnp.mean(values, axis=-1, keepdims=True)
    centred = values - average
    spread = jnp.mean(centred * centred, axis=-1, keepdims=True)
    return centred * lax.rsqrt(spread + norm_eps) * gain_vec + shift_vec


def gelu_tanh(values):
    return jax.nn.gelu(values, approximate=True)


def dot(a, b, contract):
    return lax.dot_general(a, b, ((contract[:1], contract[1:]), ((), ())), preferred_element_type=F32)


def project_kernel(seqs, halves, pairs, x_ref, gain_ref, shift_ref, w_ref, *refs):
    out_refs, normed_ref = refs[:pairs], refs[pairs]
    rows = x_ref.shape[0] // seqs

    @pl.when(pl.program_id(0) == 0)
    def _():
        normed_ref[...] = norm_rows(x_ref[...].astype(F32), gain_ref[...], shift_ref[...]).astype(BF16)

    part = jnp.dot(normed_ref[...], w_ref[...], preferred_element_type=F32).astype(BF16)
    for pair in range(pairs):
        for half in range(halves):
            col = (half * pairs + pair) * PAIR
            for seq in range(seqs):
                out_refs[pair][half * seqs + seq] = part[seq * rows : (seq + 1) * rows, col : col + PAIR]


def project(x, gain, shift, w_qkv, halves):
    seqs, rows, width = x.shape
    pairs = width // PAIR // halves
    tokens = seqs * rows
    outs = [jax.ShapeDtypeStruct((halves * seqs, rows, 3 * PAIR), BF16)] * pairs
    whole = lambda g: (0, 0)
    return pl.pallas_call(
        functools.partial(project_kernel, seqs, halves, pairs),
        grid=(3,),
        in_specs=[
            pl.BlockSpec((tokens, width), whole),
            pl.BlockSpec((1, width), whole),
            pl.BlockSpec((1, width), whole),
            pl.BlockSpec((width, width), lambda g: (0, g)),
        ],
        out_specs=[pl.BlockSpec((halves * seqs, rows, PAIR), lambda g: (0, 0, g))] * pairs
        + [pl.BlockSpec((tokens, width), whole)],
        out_shape=outs + [jax.ShapeDtypeStruct((tokens, width), BF16)],
        cost_estimate=pl.CostEstimate(
            flops=6 * tokens * width * width, bytes_accessed=9 * width * width, transcendentals=0
        ),
        name="project",
    )(x.reshape(tokens, width), gain[None], shift[None], w_qkv)


def head_lanes(values, head):
    lane = lax.broadcasted_iota(jnp.int32, values.shape, 1)
    mine = lane < HEAD if head == 0 else lane >= HEAD
    return jnp.where(mine, values, jnp.zeros_like(values))


def gather_rows(place_ref, source_ref, columns, target_ref):
    blocks, rows = source_ref.shape[0], source_ref.shape[1]
    for block in range(blocks):
        at = pl.multiple_of(place_ref[block] * rows, rows)
        target_ref[pl.ds(at, rows), :] = source_ref[block, :, columns]


def scatter_rows(place_ref, source_ref, target_ref, columns):
    blocks, rows = target_ref.shape[0], target_ref.shape[1]
    for block in range(blocks):
        at = pl.multiple_of(place_ref[block] * rows, rows)
        target_ref[block, :, columns] = source_ref[pl.ds(at, rows), :].astype(target_ref.dtype)


def hide_later(magnitude):
    keys = magnitude.shape[0]
    key = lax.broadcasted_iota(jnp.int32, (QTILE, QTILE), 0)
    query = lax.broadcasted_iota(jnp.int32, (QTILE, QTILE), 1)
    last = jnp.where(key <= query, magnitude[keys - QTILE :], HIDDEN)
    return last if keys == QTILE else jnp.concatenate([magnitude[: keys - QTILE], last], axis=0)


def sign_of(scores):
    return jnp.clip(scores * HUGE, -1.0, 1.0)


def attend_kernel(place_ref, x_ref, out_ref, sums_ref, stats_ref, q_sc, k_sc, v_sc, o_sc):
    gather_rows(place_ref, x_ref, slice(0, PAIR), q_sc)
    gather_rows(place_ref, x_ref, slice(PAIR, 2 * PAIR), k_sc)
    gather_rows(place_ref, x_ref, slice(2 * PAIR, 3 * PAIR), v_sc)
    total_rows = q_sc.shape[0]
    v_t = v_sc[...].T
    for tile in range(total_rows // QTILE):
        span = slice(tile * QTILE, (tile + 1) * QTILE)
        keys = (tile + 1) * QTILE
        queries = q_sc[span, :] * SCALE
        for head in range(2):
            scores = dot(k_sc[:keys, :], head_lanes(queries, head).astype(BF16), (1, 1))
            magnitude = hide_later(jnp.abs(scores))
            peak = jnp.max(magnitude, axis=0, keepdims=True)
            exponents = jnp.exp(magnitude - peak)
            total = jnp.sum(exponents, axis=0, keepdims=True)
            weights = (exponents * sign_of(scores)).astype(BF16)
            summed = dot(v_t[head * HEAD : (head + 1) * HEAD, :keys], weights, (1, 0))
            sums_ref[head * HEAD : (head + 1) * HEAD, span] = summed / total
            stats_ref[head : head + 1, span] = peak + jnp.log(total)
        o_sc[span, :] = sums_ref[:, span].T
    scatter_rows(place_ref, o_sc, out_ref, slice(None))


def attend(place, x):
    blocks, rows, _ = x.shape
    length = blocks * rows
    area = length * length
    return pl.pallas_call(
        attend_kernel,
        grid_spec=pltpu.PrefetchScalarGridSpec(
            num_scalar_prefetch=1,
            grid=(1,),
            in_specs=[pl.BlockSpec(x.shape, lambda i, p: (0, 0, 0))],
            out_specs=[
                pl.BlockSpec((blocks, rows, PAIR), lambda i, p: (0, 0, 0)),
                pl.BlockSpec((PAIR, length), lambda i, p: (0, 0)),
                pl.BlockSpec((8, length), lambda i, p: (0, 0)),
            ],
            scratch_shapes=[pltpu.VMEM((length, PAIR), BF16)] * 3 + [pltpu.VMEM((length, PAIR), F32)],
        ),
        out_shape=[
            jax.ShapeDtypeStruct((blocks, rows, PAIR), BF16),
            jax.ShapeDtypeStruct((PAIR, length), F32),
            jax.ShapeDtypeStruct((8, length), F32),
        ],
        cost_estimate=pl.CostEstimate(
            flops=16 * area * HEAD, bytes_accessed=4 * length * PAIR * 4, transcendentals=area
        ),
        name="attend",
    )(place, x)


def attend_back_kernel(
    place_ref, x_ref, g_ref, sums_ref, stats_ref, out_ref, q_sc, k_sc, v_sc, g_sc, dq_sc, dk_sc, dv_sc
):
    gather_rows(place_ref, x_ref, slice(0, PAIR), q_sc)
    gather_rows(place_ref, x_ref, slice(PAIR, 2 * PAIR), k_sc)
    gather_rows(place_ref, x_ref, slice(2 * PAIR, 3 * PAIR), v_sc)
    gather_rows(place_ref, g_ref, slice(0, PAIR), g_sc)
    total_rows = q_sc.shape[0]
    k_t = k_sc[...].T
    g_t = g_sc[...].astype(F32).T
    products = g_t * sums_ref[...]
    deltas = [
        jnp.sum(products[head * HEAD : (head + 1) * HEAD], axis=0, keepdims=True) for head in range(2)
    ]
    dk_sc[...] = jnp.zeros_like(dk_sc)
    dv_sc[...] = jnp.zeros_like(dv_sc)
    for tile in range(total_rows // QTILE):
        span = slice(tile * QTILE, (tile + 1) * QTILE)
        keys = (tile + 1) * QTILE
        queries = q_sc[span, :] * SCALE
        parts = []
        for head in range(2):
            q_head = head_lanes(queries, head).astype(BF16)
            g_head = head_lanes(g_sc[span, :], head)
            scores = dot(k_sc[:keys, :], q_head, (1, 1))
            magnitude = hide_later(jnp.abs(scores))
            sign = sign_of(scores)
            signed = jnp.exp(magnitude - stats_ref[head : head + 1, span]) * sign
            grad_weights = dot(v_sc[:keys, :], g_head, (1, 1))
            grad_scores = (signed * (sign * grad_weights - deltas[head][:, span])).astype(BF16)
            dv_sc[:keys, :] += dot(signed.astype(BF16), g_head, (1, 0))
            dk_sc[:keys, :] += dot(grad_scores, q_head, (1, 0))
            parts.append(dot(k_t[head * HEAD : (head + 1) * HEAD, :keys], grad_scores, (1, 0)))
        dq_sc[span, :] = jnp.concatenate(parts, axis=0).T * SCALE
    scatter_rows(place_ref, dq_sc, out_ref, slice(0, PAIR))
    scatter_rows(place_ref, dk_sc, out_ref, slice(PAIR, 2 * PAIR))
    scatter_rows(place_ref, dv_sc, out_ref, slice(2 * PAIR, 3 * PAIR))


def attend_back(place, x, grad, sums, stats):
    blocks, rows, _ = x.shape
    length = blocks * rows
    area = length * length
    block3 = lambda i, p: (0, 0, 0)
    block2 = lambda i, p: (0, 0)
    return pl.pallas_call(
        attend_back_kernel,
        grid_spec=pltpu.PrefetchScalarGridSpec(
            num_scalar_prefetch=1,
            grid=(1,),
            in_specs=[
                pl.BlockSpec(x.shape, block3),
                pl.BlockSpec(grad.shape, block3),
                pl.BlockSpec(sums.shape, block2),
                pl.BlockSpec(stats.shape, block2),
            ],
            out_specs=pl.BlockSpec(x.shape, block3),
            scratch_shapes=[pltpu.VMEM((length, PAIR), BF16)] * 4 + [pltpu.VMEM((length, PAIR), F32)] * 3,
        ),
        out_shape=jax.ShapeDtypeStruct(x.shape, BF16),
        cost_estimate=pl.CostEstimate(
            flops=40 * area * HEAD, bytes_accessed=8 * length * PAIR * 4, transcendentals=area
        ),
        name="attend_back",
    )(place, x, grad, sums, stats)


def exchange(blocks):
    return lax.all_to_all(blocks, ("pb", "ka"), 0, 0, tiled=True)


def shards(
    inputs,
    block_place,
    ln1_gain,
    ln1_shift,
    w_qkv,
    w_out,
    ln2_gain,
    ln2_shift,
    w_up,
    w_down,
    cotangent,
):
    seqs, rows, width = inputs.shape
    halves = lax.axis_size("pb")
    pairs = width // PAIR // halves
    place = lax.dynamic_index_in_dim(block_place, lax.axis_index("ka"), 0, False)
    *sent, normed1 = project(inputs, ln1_gain, ln1_shift, w_qkv, halves)
    normed1 = normed1.reshape(seqs, rows, width)
    packed = [exchange(s) for s in sent]
    attended, saved = [], []
    for x in packed:
        out, sums, stats = attend(place, x)
        saved.append((sums, stats))
        attended.append(exchange(out))

    def join(pieces):
        stacked = jnp.stack(pieces)
        kinds = stacked.shape[-1] // PAIR
        stacked = stacked.reshape(pairs, halves, seqs, rows, kinds, PAIR)
        return stacked.transpose(2, 3, 4, 1, 0, 5).reshape(seqs, rows, kinds * width)

    def split(whole):
        cut = whole.reshape(seqs, rows, halves, pairs, PAIR).transpose(3, 2, 0, 1, 4)
        return [cut[p].reshape(halves * seqs, rows, PAIR) for p in range(pairs)]

    attended = join(attended)
    source = inputs.astype(jnp.float32)
    residual = source + jnp.einsum(
        "btd,de->bte", attended, w_out, preferred_element_type=jnp.float32
    )
    normed2, second_back = jax.vjp(norm_rows, residual, ln2_gain, ln2_shift)
    normed2 = normed2.astype(jnp.bfloat16)
    pre_act = jnp.einsum("btd,df->btf", normed2, w_up, preferred_element_type=jnp.float32)
    active, gelu_back = jax.vjp(gelu_tanh, pre_act)
    active = active.astype(jnp.bfloat16)
    outputs = (
        residual + jnp.einsum("btf,fd->btd", active, w_down, preferred_element_type=jnp.float32)
    ).astype(jnp.bfloat16)
    grad_down = jnp.einsum("btf,btd->fd", active, cotangent, preferred_element_type=jnp.float32)
    grad_act = jnp.einsum("btd,fd->btf", cotangent, w_down, preferred_element_type=jnp.float32)
    grad_pre = gelu_back(grad_act)[0].astype(jnp.bfloat16)
    grad_up = jnp.einsum("btd,btf->df", normed2, grad_pre, preferred_element_type=jnp.float32)
    grad_normed2 = jnp.einsum("btf,df->btd", grad_pre, w_up, preferred_element_type=jnp.float32)
    grad_res, grad_gain2, grad_shift2 = second_back(grad_normed2)
    grad_res = grad_res + cotangent.astype(jnp.float32)
    grad_z = grad_res.astype(jnp.bfloat16)
    grad_proj = jnp.einsum("btd,bte->de", attended, grad_z, preferred_element_type=jnp.float32)
    grad_att = jnp.einsum("bte,de->btd", grad_z, w_out, preferred_element_type=jnp.float32).astype(
        jnp.bfloat16
    )
    grads = []
    for x, g, (sums, stats) in zip(packed, split(grad_att), saved):
        grads.append(exchange(attend_back(place, x, exchange(g), sums, stats)))
    grad_packed = join(grads)
    grad_qkv = jnp.einsum("btd,bte->de", normed1, grad_packed, preferred_element_type=jnp.float32)
    grad_normed1 = jnp.einsum("bte,de->btd", grad_packed, w_qkv, preferred_element_type=jnp.float32)
    _, first_back = jax.vjp(norm_rows, source, ln1_gain, ln1_shift)
    grad_source, grad_gain1, grad_shift1 = first_back(grad_normed1)
    grad_inputs = (grad_res + grad_source).astype(jnp.bfloat16)
    norm_local = jnp.stack([grad_gain1, grad_shift1, grad_gain2, grad_shift2])

    def scatter(g):
        g = lax.psum_scatter(g.astype(BF16), "batch", scatter_dimension=0, tiled=True)
        return lax.psum_scatter(g, ("pb", "ka"), scatter_dimension=1, tiled=True).astype(F32)

    norm_sum = lax.psum(
        lax.psum_scatter(norm_local, ("pb", "ka"), scatter_dimension=1, tiled=True), "batch"
    )
    return (
        outputs,
        grad_inputs,
        scatter(grad_qkv),
        scatter(grad_proj),
        scatter(grad_up),
        scatter(grad_down),
        norm_sum,
    )


def solution(mesh):
    placed = (
        P("batch", ("pb", "ka"), None),
        P("batch", None),
        P(),
        P(),
        P(),
        P(),
        P(),
        P(),
        P(),
        P(),
        P("batch", ("pb", "ka"), None),
    )
    return jax.shard_map(
        shards,
        mesh=mesh,
        in_specs=placed,
        out_specs=(
            P("batch", ("pb", "ka"), None),
            P("batch", ("pb", "ka"), None),
            P("batch", ("pb", "ka")),
            P("batch", ("pb", "ka")),
            P("batch", ("pb", "ka")),
            P("batch", ("pb", "ka")),
            P(None, ("pb", "ka")),
        ),
        check_vma=False,
    )
```

time: 967 us -> 669 us (0.69)
  waiting for transfers between devices: 639 us -> 407 us
  matrix products: 160 us -> 52.4 us
  Pallas kernels: 0 us -> 49.2 us
  other arithmetic: 55.3 us -> 7.7 us
  starting transfers between devices: 2.39 us -> 48.9 us
  local copies, waits for them, and re-layouts: 60.4 us -> 40.1 us
  blocking collectives: 26.9 us -> 44.3 us
    reduce_scatter x8 -> x4, waiting for transfers between devices: 341 us -> 211 us  [scatter(): lax.psum_scatter(g.astype(BF16), 'batch', scatter_dimension=0, tiled=True)]
    all_gather x4 -> x0, waiting for transfers between devices: 108 us -> none  [the longest x1 28.1 us: shards(): grad_half = lax.all_gather(grad_att, 'ka', axis=1, tiled=True)]
    dot_general x7 -> x0, matrix products: 102 us -> none  [the longest x1 27 us: shards(): jnp.einsum('bqhe,bkhe->bhqk', grad_heads, value_heads, preferred_element_...]
    pallas_call x0 -> x7, Pallas kernels: none -> 49.2 us  [the longest x3 21.9 us: attend(): pl.pallas_call(attend_kernel, grid_spec=pltpu.PrefetchScalarGridSpec(num_...]
    all_to_all x0 -> x10, starting transfers between devices: none -> 48.2 us  [exchange(): return lax.all_to_all(blocks, ('pb', 'ka'), 0, 0, tiled=True)]
    all_to_all x0 -> x2, blocking collectives: none -> 32.1 us  [exchange(): return lax.all_to_all(blocks, ('pb', 'ka'), 0, 0, tiled=True)]
    all_to_all x0 -> x10, waiting for transfers between devices: none -> 32 us  [exchange(): return lax.all_to_all(blocks, ('pb', 'ka'), 0, 0, tiled=True)]
    psum x1 -> x0, waiting for transfers between devices: 31.7 us -> none  [shards(): delta_rows = lax.psum(jnp.sum(signed * grad_weights, axis=-1), 'ka')]
  transfers between devices with their start and end apart: 18 -> 19, of which waited for: 17 -> 15; matrix products, arithmetic and copies ran while one was open for 12% -> 10% of each run, Pallas kernels for 0% -> 6%
where the time goes in v1:
time: 669 us; the launch traced here: 664 us
  waiting for transfers between devices  407 us (61%)
  matrix products  52.4 us (8%)
  Pallas kernels  49.2 us (7%)
  starting transfers between devices  48.9 us (7%)
  blocking collectives  44.3 us (7%)
  local copies, waits for them, and re-layouts  40.1 us (6%)
  between operations  14.6 us (2%)
  other arithmetic  7.7 us (1%)
    reduce_scatter x4, waiting for transfers between devices, scatter(): lax.psum_scatter(g.astype(BF16), 'batch', scatter_dimension=0, tiled=True)  211 us
    unnamed x14, waiting for transfers between devices  165 us
    all_to_all x10, starting transfers between devices, exchange(): return lax.all_to_all(blocks, ('pb', 'ka'), 0, 0, tiled=True)  48.2 us
    all_to_all x2, blocking collectives, exchange(): return lax.all_to_all(blocks, ('pb', 'ka'), 0, 0, tiled=True)  32.1 us
    all_to_all x10, waiting for transfers between devices, exchange(): return lax.all_to_all(blocks, ('pb', 'ka'), 0, 0, tiled=True)  32 us
    unnamed x77, local copies, waits for them, and re-layouts  22.6 us
    pallas_call x3, Pallas kernels, attend(): pl.pallas_call(attend_kernel, grid_spec=pltpu.PrefetchScalarGridSpec(num_...  21.9 us
    pallas_call x3, Pallas kernels, attend_back(): pl.pallas_call(attend_back_kernel, grid_spec=pltpu.PrefetchScalarGridSpec...  21.3 us
  transfers between devices with their start and end apart: 19, of which 15 were waited for; matrix products, arithmetic and copies ran while one was open for 10% of the time, Pallas kernels for 6%

profile of v1, /device:TPU:0, one launch (start us, length us, event | category | flops | bytes accessed | tf_op | source)
XLA Modules:
  0.0 664.4 jit_solution(12351705025547976466)
XLA Ops:
  7.2 1.4 broadcast_in_dim.12.gain_ref
  8.5 1.3 broadcast_in_dim.26.shift_ref
  9.8 6.1 project.1
  15.9 17.2 %all_to_all.60.x_ref = bf16[8,128,384]{2,1,0:T(8,128)(2,1)} all-to-all(bf16[8,128,384]{2,1,0:T(8,128)(2,1)} %get-tuple-element.24), channel_id=1, replica_groups=mesh['batch'=4,'pb'=2,'ka'=4] {'pb','ka'}, dimensions={0} | all-to-all | bytes 1572864 | tf_op jit(solution)/shard_map/all_to_all | solution.py:232
  33.1 14.9 %all_to_all.61.x_ref = bf16[8,128,384]{2,1,0:T(8,128)(2,1)} all-to-all(bf16[8,128,384]{2,1,0:T(8,128)(2,1)S(1)} %copy-done.14), channel_id=1, replica_groups=mesh['batch'=4,'pb'=2,'ka'=4] {'pb','ka'}, dimensions={0} | all-to-all | bytes 1572864 | tf_op jit(solution)/shard_map/all_to_all | solution.py:232
  48.0 3.5 all-to-all-start
  51.5 1.2 dynamic-slice_bitcast_fusion.place_ref
  52.7 7.3 %attend.5 = (bf16[8,128,128]{2,1,0:T(8,128)(2,1)}, f32[128,1024]{1,0:T(8,128)}, f32[8,1024]{1,0:T(8,128)}) custom-call(s32[8]{0:T(128)} %dynamic-slice_bitcast_fusion.place_ref, bf16[8,128,384]{2,1,0:T(8,128)(2,1)} %all_to_all.60.x_ref), custom_call_target="tpu_custom_call" | custom-call | flops 1073741824 | bytes 2097152 | tf_op jit(solution)/shard_map/attend/pallas_call | solution.py:139
  60.0 3.1 all-to-all-done.x_ref
  63.1 3.4 all-to-all-start.5
  66.6 7.3 %attend.4 = (bf16[8,128,128]{2,1,0:T(8,128)(2,1)}, f32[128,1024]{1,0:T(8,128)}, f32[8,1024]{1,0:T(8,128)}) custom-call(s32[8]{0:T(128)} %dynamic-slice_bitcast_fusion.place_ref, bf16[8,128,384]{2,1,0:T(8,128)(2,1)} %all_to_all.61.x_ref), custom_call_target="tpu_custom_call" | custom-call | flops 1073741824 | bytes 2097152 | tf_op jit(solution)/shard_map/attend/pallas_call | solution.py:139
  73.9 13.6 %all-to-all-start.3 = ((bf16[8,128,128]{2,1,0:T(8,128)(2,1)}), bf16[8,128,128]{2,1,0:T(8,128)(2,1)S(1)}, u32[]{:S(2)}, u32[]{:S(2)}) async-start(bf16[8,128,128]{2,1,0:T(8,128)(2,1)} %get-tuple-element.23), calls=%async_computation.3 | async-start | bytes 524288 | tf_op jit(solution)/shard_map/all_to_all | solution.py:232
  87.4 7.3 %attend.3 = (bf16[8,128,128]{2,1,0:T(8,128)(2,1)}, f32[128,1024]{1,0:T(8,128)}, f32[8,1024]{1,0:T(8,128)}) custom-call(s32[8]{0:T(128)} %dynamic-slice_bitcast_fusion.place_ref, bf16[8,128,384]{2,1,0:T(8,128)(2,1)} %copy-done.13), custom_call_target="tpu_custom_call" | custom-call | flops 1073741824 | bytes 2097152 | tf_op jit(solution)/shard_map/attend/pallas_call | solution.py:139
  94.7 4.2 all-to-all-start.1
  99.3 5.7 all-to-all-done.1
  107.0 5.0 fusion.13
  112.1 6.1 fusion.6
  118.2 3.0 multiply_reduce_fusion
  124.0 1.7 convolution_convert_fusion
  125.7 1.5 copy.48
  128.0 1.8 copy.53
  129.8 3.4 all-to-all-start.10
  133.3 1.8 copy.51
  135.0 4.3 all-to-all-done.10.g_ref
  139.3 3.4 all-to-all-start.8
  143.6 5.2 all-to-all-done.8.g_ref
  148.8 3.6 all-to-all-start.6
  152.4 7.1 %attend_back.5 = bf16[8,128,384]{2,1,0:T(8,128)(2,1)} custom-call(s32[8]{0:T(128)} %dynamic-slice_bitcast_fusion.place_ref, bf16[8,128,384]{2,1,0:T(8,128)(2,1)} %all_to_all.60.x_ref, bf16[8,128,128]{2,1,0:T(8,128)(2,1)} %copy-done.18, f32[128,1024]{1,0:T(8,128)} %get-tuple-element.30.sums_ref, f32[8,1024]{1,0:T(8,128)} %get-tuple-element.31.stats_ref), custom_call_target="tpu_custom_call" | custom-call | flops 2684354560 | bytes 4194304 | tf_op jit(solution)/shard_map/attend_back/pallas_call | solution.py:209
  159.5 4.2 all-to-all-start.11
  163.7 3.2 bitcast_convert_fusion.3
  166.9 7.1 %attend_back.4 = bf16[8,128,384]{2,1,0:T(8,128)(2,1)} custom-call(s32[8]{0:T(128)} %dynamic-slice_bitcast_fusion.place_ref, bf16[8,128,384]{2,1,0:T(8,128)(2,1)} %all_to_all.61.x_ref, bf16[8,128,128]{2,1,0:T(8,128)(2,1)} %copy-done.17, f32[128,1024]{1,0:T(8,128)} %get-tuple-element.28.sums_ref, f32[8,1024]{1,0:T(8,128)} %get-tuple-element.29.stats_ref), custom_call_target="tpu_custom_call" | custom-call | flops 2684354560 | bytes 4194304 | tf_op jit(solution)/shard_map/attend_back/pallas_call | solution.py:209
  174.0 1.3 all-to-all-done.11
  175.3 4.6 all-to-all-start.9
  180.0 7.1 %attend_back.3 = bf16[8,128,384]{2,1,0:T(8,128)(2,1)} custom-call(s32[8]{0:T(128)} %dynamic-slice_bitcast_fusion.place_ref, bf16[8,128,384]{2,1,0:T(8,128)(2,1)} %copy-done.13, bf16[8,128,128]{2,1,0:T(8,128)(2,1)} %copy-done.16, f32[128,1024]{1,0:T(8,128)} %get-tuple-element.26.sums_ref, f32[8,1024]{1,0:T(8,128)} %get-tuple-element.27.stats_ref), custom_call_target="tpu_custom_call" | custom-call | flops 2684354560 | bytes 4194304 | tf_op jit(solution)/shard_map/attend_back/pallas_call | solution.py:209
  187.1 4.5 all-to-all-done.9
  191.6 4.2 all-to-all-start.7
  195.9 1.5 copy.54
  197.4 2.3 copy.52
  199.7 7.8 %all-to-all-done.7 = bf16[8,128,384]{2,1,0:T(8,128)(2,1)} async-done(((bf16[8,128,384]{2,1,0:T(8,128)(2,1)}), bf16[8,128,384]{2,1,0:T(8,128)(2,1)}, u32[]{:S(2)}, u32[]{:S(2)}) %all-to-all-start.7) | async-done | bytes 786464 | tf_op jit(solution)/shard_map/all_to_all | solution.py:232
  207.5 2.3 copy.50
  209.8 1.6 maximum_bitcast_fusion
  211.6 1.4 copy-done.12
  213.0 3.8 bitcast_convert_fusion.2
  217.6 6.4 bitcast_convert_fusion.1
  225.2 8.3 %bitcast_convert_fusion = bf16[3072,768]{1,0:T(8,128)(2,1)} fusion(bf16[4,128,768]{2,1,0:T(8,128)(2,1)S(1)} %copy-done.10, f32[4,128,3072]{2,1,0:T(8,128)} %copy-done.27), kind=kOutput, calls=%fused_computation | convolution fusion | flops 2432434176 | bytes 11796480 | tf_op jit(solution)/shard_map/btf,btd->fd/dot_general | solution.py:284
  234.2 5.1 fusion.23
  239.3 1.1 copy-done.5
  242.3 1.9 copy.70
  244.3 39.9 %reduce-scatter.20.cloned.1.call-done = bf16[192,2304]{1,0:T(8,128)(2,1)} async-done(((bf16[768,2304]{1,0:T(8,128)(2,1)}), bf16[192,2304]{1,0:T(8,128)(2,1)}) %reduce-scatter.20.cloned.1.call-update) | async-done | bytes 884752 | tf_op jit(solution)/shard_map/reduce_scatter | solution.py:308
  284.2 2.3 copy.68
  286.6 85.4 %reduce-scatter.24.cloned.1.call-done = bf16[192,3072]{1,0:T(8,128)(2,1)} async-done(((bf16[768,3072]{1,0:T(8,128)(2,1)}), bf16[192,3072]{1,0:T(8,128)(2,1)}) %reduce-scatter.24.cloned.1.call-update) | async-done | bytes 1179664 | tf_op jit(solution)/shard_map/reduce_scatter | solution.py:308
  372.0 2.5 copy.72
  374.8 85.2 %reduce-scatter.26.cloned.1.call-done = bf16[768,768]{1,0:T(8,128)(2,1)} async-done(((bf16[3072,768]{1,0:T(8,128)(2,1)}), bf16[768,768]{1,0:T(8,128)(2,1)}) %reduce-scatter.26.cloned.1.call-update) | async-done | bytes 1179664 | tf_op jit(solution)/shard_map/reduce_scatter | solution.py:308
  460.0 2.3 copy.74
  462.4 8.9 %add_convert_fusion.1 = bf16[4,128,768]{2,1,0:T(8,128)(2,1)} fusion(f32[4,128,768]{2,1,0:T(8,128)S(1)} %get-tuple-element.70, bf16[3072,768]{1,0:T(8,128)(2,1)} %param.20, f32[4,128,3072]{2,1,0:T(8,128)} %copy-done.27), kind=kOutput, calls=%fused_computation.42 | convolution fusion | flops 2430861312 | bytes 13369344 | tf_op jit(solution)/shard_map/btf,fd->btd/dot_general | solution.py:282
  471.4 1.6 add_convert_fusion
  473.0 24.3 %reduce-scatter.36.cloned.1.call-done = f32[96,4]{1,0:T(8,128)} async-done(((f32[768,4]{1,0:T(8,128)}), f32[96,4]{1,0:T(8,128)}) %reduce-scatter.36.cloned.1.call-update) | async-done | bytes 1552
  498.2 12.2 %psum.7 = f32[4,96]{1,0:T(4,128)} all-reduce(f32[4,96]{1,0:T(4,128)S(1)} %copy.77), channel_id=1, replica_groups=mesh['batch'=4,'pb'=2,'ka'=4] {'batch'}, use_global_device_ids=true, to_apply=%region_21.22 | all-reduce | flops 384 | bytes 3072 | tf_op jit(solution)/shard_map/psum | solution.py:311
  510.4 23.7 %reduce-scatter.30.cloned.1.call-done = bf16[96,192]{1,0:T(8,128)(2,1)} async-done(((bf16[768,192]{1,0:T(8,128)(2,1)}), bf16[96,192]{1,0:T(8,128)(2,1)}) %reduce-scatter.30.cloned.1.call-update) | async-done | bytes 36880
  535.8 38.3 %reduce-scatter.28.cloned.1.call-done = bf16[288,192]{1,0:T(8,128)(2,1)} async-done(((bf16[2304,192]{1,0:T(8,128)(2,1)}), bf16[288,192]{1,0:T(8,128)(2,1)}) %reduce-scatter.28.cloned.1.call-update) | async-done | bytes 110608
  575.9 39.8 %reduce-scatter.32.cloned.1.call-done = bf16[384,192]{1,0:T(8,128)(2,1)} async-done(((bf16[3072,192]{1,0:T(8,128)(2,1)}), bf16[384,192]{1,0:T(8,128)(2,1)}) %reduce-scatter.32.cloned.1.call-update) | async-done | bytes 147472
  615.7 1.1 copy.73
  617.5 38.1 %reduce-scatter.34.cloned.1.call-done = bf16[96,768]{1,0:T(8,128)(2,1)} async-done(((bf16[768,768]{1,0:T(8,128)(2,1)}), bf16[96,768]{1,0:T(8,128)(2,1)}) %reduce-scatter.34.cloned.1.call-update) | async-done | bytes 147472
  655.7 1.1 copy.75
  (121 shorter events, 17.6 us)
Async XLA Ops:
  7.2 98.2 %copy-start = (bf16[768,768]{1,0:T(8,128)(2,1)S(1)}, bf16[768,768]{1,0:T(8,128)(2,1)}, u32[]{:S(2)}) copy-start(bf16[768,768]{1,0:T(8,128)(2,1)} %param.16) | copy-start | bytes 3538948
  15.9 17.2 %copy-start.14 = (bf16[8,128,384]{2,1,0:T(8,128)(2,1)S(1)}, bf16[8,128,384]{2,1,0:T(8,128)(2,1)}, u32[]{:S(2)}) copy-start(bf16[8,128,384]{2,1,0:T(8,128)(2,1)} %get-tuple-element.22) | copy-start | bytes 2359300
  48.0 15.1 %all-to-all-start = ((bf16[8,128,384]{2,1,0:T(8,128)(2,1)}), bf16[8,128,384]{2,1,0:T(8,128)(2,1)S(1)}, u32[]{:S(2)}, u32[]{:S(2)}) async-start(bf16[8,128,384]{2,1,0:T(8,128)(2,1)} %get-tuple-element.20), calls=%async_computation | async-start | bytes 1572864 | tf_op jit(solution)/shard_map/all_to_all | solution.py:232
  63.1 10.7 %copy-start.13 = (bf16[8,128,384]{2,1,0:T(8,128)(2,1)}, bf16[8,128,384]{2,1,0:T(8,128)(2,1)S(1)}, u32[]{:S(2)}) copy-start(bf16[8,128,384]{2,1,0:T(8,128)(2,1)S(1)} %all-to-all-done.x_ref) | copy-start | bytes 2359300
  63.1 10.7 %all-to-all-start.5 = ((bf16[8,128,128]{2,1,0:T(8,128)(2,1)}), bf16[8,128,128]{2,1,0:T(8,128)(2,1)S(1)}, u32[]{:S(2)}, u32[]{:S(2)}) async-start(bf16[8,128,128]{2,1,0:T(8,128)(2,1)} %get-tuple-element.25), calls=%async_computation.5 | async-start | bytes 524288 | tf_op jit(solution)/shard_map/all_to_all | solution.py:232
  73.9 20.9 %all-to-all-start.3 = ((bf16[8,128,128]{2,1,0:T(8,128)(2,1)}), bf16[8,128,128]{2,1,0:T(8,128)(2,1)S(1)}, u32[]{:S(2)}, u32[]{:S(2)}) async-start(bf16[8,128,128]{2,1,0:T(8,128)(2,1)} %get-tuple-element.23), calls=%async_computation.3 | async-start | bytes 524288 | tf_op jit(solution)/shard_map/all_to_all | solution.py:232
  94.7 10.3 %all-to-all-start.1 = ((bf16[8,128,128]{2,1,0:T(8,128)(2,1)}), bf16[8,128,128]{2,1,0:T(8,128)(2,1)S(1)}, u32[]{:S(2)}, u32[]{:S(2)}) async-start(bf16[8,128,128]{2,1,0:T(8,128)(2,1)} %get-tuple-element.21), calls=%async_computation.1 | async-start | bytes 524288 | tf_op jit(solution)/shard_map/all_to_all | solution.py:232
  98.9 6.4 copy-start.4
  105.3 0.9 copy-start.8
  106.3 0.7 copy-start.22
  106.3 0.7 copy-start.24
  106.3 5.7 slice-start.2
  107.0 5.0 copy-start.9
  107.0 5.1 slice-start.3
  107.0 11.2 %slice-start = ((s8[4718592]{0:T(1024)(128)(4,1)}), s8[4194304]{0:T(1024)(128)(4,1)S(1)}, s32[]{:S(2)}) async-start(s8[4718592]{0:T(1024)(128)(4,1)} %bitcast.101), calls=%async_computation.30 | async-start | bytes 8388608
  112.0 6.1 copy-start.27
  112.0 6.2 slice-start.1
  118.2 3.0 copy-start.28
  121.8 1.2 copy-start.2
  121.8 1.2 copy-start.20
  123.0 1.0 copy-start.15
  129.8 9.5 %all-to-all-start.10 = ((bf16[8,128,128]{2,1,0:T(8,128)(2,1)}), bf16[8,128,128]{2,1,0:T(8,128)(2,1)S(1)}, u32[]{:S(2)}, u32[]{:S(2)}) async-start(bf16[8,128,128]{2,1,0:T(8,128)(2,1)} %bitcast.17), calls=%async_computation.10 | async-start | bytes 524288 | tf_op jit(solution)/shard_map/all_to_all | solution.py:232
  139.3 13.1 %copy-start.18 = (bf16[8,128,128]{2,1,0:T(8,128)(2,1)}, bf16[8,128,128]{2,1,0:T(8,128)(2,1)S(1)}, u32[]{:S(2)}) copy-start(bf16[8,128,128]{2,1,0:T(8,128)(2,1)S(1)} %all-to-all-done.10.g_ref) | copy-start | bytes 786436
  139.3 9.5 %all-to-all-start.8 = ((bf16[8,128,128]{2,1,0:T(8,128)(2,1)}), bf16[8,128,128]{2,1,0:T(8,128)(2,1)S(1)}, u32[]{:S(2)}, u32[]{:S(2)}) async-start(bf16[8,128,128]{2,1,0:T(8,128)(2,1)} %bitcast.15), calls=%async_computation.8 | async-start | bytes 524288 | tf_op jit(solution)/shard_map/all_to_all | solution.py:232
  148.8 10.7 %copy-start.17 = (bf16[8,128,128]{2,1,0:T(8,128)(2,1)}, bf16[8,128,128]{2,1,0:T(8,128)(2,1)S(1)}, u32[]{:S(2)}) copy-start(bf16[8,128,128]{2,1,0:T(8,128)(2,1)S(1)} %all-to-all-done.8.g_ref) | copy-start | bytes 786436
  148.8 10.7 %all-to-all-start.6 = ((bf16[8,128,128]{2,1,0:T(8,128)(2,1)}), bf16[8,128,128]{2,1,0:T(8,128)(2,1)S(1)}, u32[]{:S(2)}, u32[]{:S(2)}) async-start(bf16[8,128,128]{2,1,0:T(8,128)(2,1)} %bitcast.12), calls=%async_computation.6 | async-start | bytes 524288 | tf_op jit(solution)/shard_map/all_to_all | solution.py:232
  159.5 7.4 %copy-start.16 = (bf16[8,128,128]{2,1,0:T(8,128)(2,1)}, bf16[8,128,128]{2,1,0:T(8,128)(2,1)S(1)}, u32[]{:S(2)}) copy-start(bf16[8,128,128]{2,1,0:T(8,128)(2,1)S(1)} %all-to-all-done.6.g_ref) | copy-start | bytes 786436
  159.5 15.8 %all-to-all-start.11 = ((bf16[8,128,384]{2,1,0:T(8,128)(2,1)}), bf16[8,128,384]{2,1,0:T(8,128)(2,1)S(1)}, u32[]{:S(2)}, u32[]{:S(2)}) async-start(bf16[8,128,384]{2,1,0:T(8,128)(2,1)} %attend_back.5), calls=%async_computation.11 | async-start | bytes 1572864 | tf_op jit(solution)/shard_map/all_to_all | solution.py:232
  163.7 78.7 %reduce-scatter.22.cloned.1.call-start = ((), (), s32[]{:S(2)}) async-start(), calls=%async_computation.22 | async-start | bytes 1474560 | tf_op jit(solution)/shard_map/reduce_scatter | solution.py:308
  175.3 11.8 %copy-start.7 = (bf16[8,128,384]{2,1,0:T(8,128)(2,1)}, bf16[8,128,384]{2,1,0:T(8,128)(2,1)S(1)}, u32[]{:S(2)}) copy-start(bf16[8,128,384]{2,1,0:T(8,128)(2,1)S(1)} %all-to-all-done.11) | copy-start | bytes 2359300
  175.3 16.3 %all-to-all-start.9 = ((bf16[8,128,384]{2,1,0:T(8,128)(2,1)}), bf16[8,128,384]{2,1,0:T(8,128)(2,1)}, u32[]{:S(2)}, u32[]{:S(2)}) async-start(bf16[8,128,384]{2,1,0:T(8,128)(2,1)} %attend_back.4), calls=%async_computation.9 | async-start | bytes 1572864 | tf_op jit(solution)/shard_map/all_to_all | solution.py:232
  191.6 15.9 %all-to-all-start.7 = ((bf16[8,128,384]{2,1,0:T(8,128)(2,1)}), bf16[8,128,384]{2,1,0:T(8,128)(2,1)}, u32[]{:S(2)}, u32[]{:S(2)}) async-start(bf16[8,128,384]{2,1,0:T(8,128)(2,1)} %attend_back.3), calls=%async_computation.7 | async-start | bytes 1572864 | tf_op jit(solution)/shard_map/all_to_all | solution.py:232
  195.8 88.4 %reduce-scatter.20.cloned.1.call-start = ((), (), s32[]{:S(2)}) async-start(), calls=%async_computation.21 | async-start | bytes 4423680 | tf_op jit(solution)/shard_map/reduce_scatter | solution.py:308
  211.4 1.6 copy-start.26
  211.6 1.4 copy-start.12
  216.9 0.7 copy-start.23
  216.9 0.7 copy-start.25
  216.9 155.1 %reduce-scatter.24.cloned.1.call-start = ((), (), s32[]{:S(2)}) async-start(), calls=%async_computation.23 | async-start | bytes 5898240 | tf_op jit(solution)/shard_map/reduce_scatter | solution.py:308
  224.0 1.2 copy-start.10
  224.0 236.0 %reduce-scatter.26.cloned.1.call-start = ((), (), s32[]{:S(2)}) async-start(), calls=%async_computation.24 | async-start | bytes 5898240 | tf_op jit(solution)/shard_map/reduce_scatter | solution.py:308
  233.5 0.7 copy-start.19
  233.5 263.8 %reduce-scatter.36.cloned.1.call-start = ((), (), s32[]{:S(2)}) async-start(), calls=%async_computation.29 | async-start | bytes 442368
  239.3 1.2 copy-start.5
  242.3 291.9 %reduce-scatter.30.cloned.1.call-start = ((), (), s32[]{:S(2)}) async-start(), calls=%async_computation.26 | async-start | bytes 442368
  244.2 329.9 %reduce-scatter.28.cloned.1.call-start = ((), (), s32[]{:S(2)}) async-start(), calls=%async_computation.25 | async-start | bytes 1327104
  286.5 329.2 %reduce-scatter.32.cloned.1.call-start = ((), (), s32[]{:S(2)}) async-start(), calls=%async_computation.27 | async-start | bytes 1769472
  374.6 281.1 %reduce-scatter.34.cloned.1.call-start = ((), (), s32[]{:S(2)}) async-start(), calls=%async_computation.28 | async-start | bytes 1327104
  462.4 9.0 %copy-start.3 = (f32[4,128,768]{2,1,0:T(8,128)S(1)}, f32[4,128,768]{2,1,0:T(8,128)}, u32[]{:S(2)}) copy-start(f32[4,128,768]{2,1,0:T(8,128)} %copy-done.2) | copy-start | bytes 4718596
  462.4 9.0 %copy-start.6 = (f32[4,128,768]{2,1,0:T(8,128)S(1)}, f32[4,128,768]{2,1,0:T(8,128)}, u32[]{:S(2)}) copy-start(f32[4,128,768]{2,1,0:T(8,128)} %copy-done.5) | copy-start | bytes 4718596
  462.4 8.9 %copy-start.11 = (bf16[4,128,768]{2,1,0:T(8,128)(2,1)S(1)}, bf16[4,128,768]{2,1,0:T(8,128)(2,1)}, u32[]{:S(2)}) copy-start(bf16[4,128,768]{2,1,0:T(8,128)(2,1)} %param.21) | copy-start | bytes 2359300
  462.4 8.9 %copy-start.21 = (f32[4,128]{1,0:T(4,128)S(1)}, f32[4,128]{1,0:T(4,128)}, u32[]{:S(2)}) copy-start(f32[4,128]{1,0:T(4,128)} %copy-done.20) | copy-start | bytes 6148
  471.4 186.2 %copy-start.1 = (bf16[768,768]{1,0:T(8,128)(2,1)S(1)}, bf16[768,768]{1,0:T(8,128)(2,1)}, u32[]{:S(2)}) copy-start(bf16[768,768]{1,0:T(8,128)(2,1)} %param.16) | copy-start | bytes 3538948
Sparse Core Ops, SparseCore 0:
  167.0 31.3 reduce-scatter.21
  217.0 67.1 reduce-scatter.19
  286.5 85.4 reduce-scatter.23
  374.2 85.7 reduce-scatter.25
  462.9 34.3 reduce-scatter.35
  500.3 33.8 reduce-scatter.29
  537.4 36.6 reduce-scatter.27
  577.4 38.2 reduce-scatter.31
  619.0 36.6 reduce-scatter.33
